TPU v7x, 512 devices: a whole 4x8x8 slice. The times are simulated.
512 devices in a mesh: seq: 64 (over z, y), req: 8 (over x, core).
Axes of the slice: x: 4, y: 8, z: 8, core: 2. Of those that a mesh axis runs over, the one named last changes fastest.
Arguments:
- hidden_in: bfloat16 [128, 4, 2048], P('req'), may hold values from -6 to 6
- attn_gain: float32 [2048], replicated, may hold values from 0.5 to 1.5
- q_gain: float32 [256], replicated, may hold values from 0.5 to 1.5
- k_gain: float32 [256], replicated, may hold values from 0.5 to 1.5
- post_attn_gain: float32 [2048], replicated, may hold values from 0.5 to 1.5
- ffn_gain: float32 [2048], replicated, may hold values from 0.5 to 1.5
- post_ffn_gain: float32 [2048], replicated, may hold values from 0.5 to 1.5
- w_qkv: bfloat16 [2048, 3072], P('seq', 'req'), may hold values from -0.125 to 0.125
- w_out: bfloat16 [2048, 2048], P('seq', 'req'), may hold values from -0.125 to 0.125
- w_gate: bfloat16 [2048, 8192], P('req', 'seq'), may hold values from -0.125 to 0.125
- w_up: bfloat16 [2048, 8192], P('req', 'seq'), may hold values from -0.125 to 0.125
- w_down: bfloat16 [8192, 2048], P('seq', 'req'), may hold values from -0.0625 to 0.0625
- prompt_keys: bfloat16 [16, 8192, 512], P('req', 'seq')
- prompt_values: bfloat16 [16, 8192, 512], P('req', 'seq'), may hold values from -6 to 6
- tail_keys: bfloat16 [8, 16384, 512], P('req', 'seq')
- tail_values: bfloat16 [8, 16384, 512], P('req', 'seq'), may hold values from -6 to 6
- group_of: int32 [128], P('req'), may hold values from 0 to 15, as said below
- prompt_lengths: int32 [16], P('req'), may hold values from 1 to 8192
- tail_lengths: int32 [128], P('req'), may hold values from 1 to 1024
- page_table: int32 [8, 1024], P('req'), may hold values from 0 to 1023, each once within a row
Outputs:
- layer_out: bfloat16 [128, 4, 2048], P('req')
Inputs may be any that keep to these rules, and one draw needn't show every extreme that they name: `group_of`: request i belongs to one of the 2 groups i // 16 * 2 to i // 16 * 2 + 1 of its own block of requests. `page_table`: each row lists every pool page of its index of req once; entry j * 64 + p is the pool page of page p of the j-th request of that block.
All inputs are finite; a program needn't handle non-finite values.
Results may differ from a plain program's by a relative error of at most 0.012.
The roundings to bfloat16 on the way count: a program that leaves them out, or rounds other values in their place, can miss the bound.
Values may be sent and summed in bfloat16 or wider, within the bound.
A program may use at most 128 MiB of HBM per device.

v0:
```python
import jax
import jax.numpy as jnp
from jax import lax
from jax.sharding import PartitionSpec as P

D = 2048
H = 8
KV = 2
HD = 256
PAGE = 16
QKV = 3072
EPSILON = 1e-06
NEGATIVE = -1e30


def normalize(values):
    return values * lax.rsqrt(jnp.mean(values * values, axis=-1, keepdims=True) + EPSILON)


def on_device(
    hidden_in,
    attn_gain,
    q_gain,
    k_gain,
    post_attn_gain,
    ffn_gain,
    post_ffn_gain,
    w_qkv,
    w_out,
    w_gate,
    w_up,
    w_down,
    prompt_keys,
    prompt_values,
    tail_keys,
    tail_values,
    group_of,
    prompt_lengths,
    tail_lengths,
    page_table,
):
    seq_index = lax.axis_index("seq")
    rows_req = hidden_in.shape[0]
    step_count = hidden_in.shape[1]
    group_size = H // KV
    tokens = rows_req * step_count
    hidden = hidden_in.astype(jnp.float32)
    normed = (normalize(hidden) * attn_gain).astype(jnp.bfloat16)
    in_rows = w_qkv.shape[0]
    normed_cols = lax.dynamic_slice_in_dim(normed, seq_index * in_rows, in_rows, 2).reshape(
        tokens, in_rows
    )
    qkv_full, out_full, gate_full, up_full, down_full = (
        lax.all_gather(w_qkv, "req", axis=1, tiled=True),
        lax.all_gather(w_out, "req", axis=1, tiled=True),
        lax.all_gather(w_gate, "req", axis=0, tiled=True),
        lax.all_gather(w_up, "req", axis=0, tiled=True),
        lax.all_gather(w_down, "req", axis=1, tiled=True),
    )
    qkv_part = jnp.dot(normed_cols, qkv_full, preferred_element_type=jnp.float32)
    projected = lax.psum(qkv_part, "seq").reshape(rows_req, step_count, QKV)
    queries = (
        normalize(projected[..., : H * HD].reshape(rows_req, step_count, H, HD)) * q_gain
    ).astype(jnp.bfloat16)
    keys_new = (
        normalize(projected[..., H * HD : (H + KV) * HD].reshape(rows_req, step_count, KV, HD))
        * k_gain
    ).astype(jnp.bfloat16)
    values_new = normalize(
        projected[..., (H + KV) * HD :].reshape(rows_req, step_count, KV, HD)
    ).astype(jnp.bfloat16)
    query_groups = queries.reshape(rows_req, step_count, KV, group_size, HD)
    group_count = prompt_keys.shape[0]
    prompt_span = prompt_keys.shape[1]
    cache_keys = prompt_keys.reshape(group_count, prompt_span, KV, HD)
    cache_values = prompt_values.reshape(group_count, prompt_span, KV, HD)
    member = (group_of % group_count)[:, None] == jnp.arange(group_count, dtype=jnp.int32)[None, :]
    prompt_pos = seq_index * prompt_span + jnp.arange(prompt_span, dtype=jnp.int32)
    prompt_live = prompt_pos[None, :] < prompt_lengths[:, None]
    prompt_mask = (member[:, :, None] & prompt_live[None, :, :])[:, None, None, None, :, :]
    prompt_scores = jnp.einsum(
        "rskgd,cpkd->rskgcp", query_groups, cache_keys, preferred_element_type=jnp.float32
    )
    prompt_scores = jnp.where(prompt_mask, prompt_scores, NEGATIVE)
    pool_rows = tail_keys.shape[1]
    slot_count = pool_rows // PAGE
    table_row = page_table[0]
    table_len = table_row.shape[0]
    tail_pages = table_len // rows_req
    slot_ids = seq_index * slot_count + jnp.arange(slot_count, dtype=jnp.int32)
    matches = table_row[None, :] == slot_ids[:, None]
    entries = jnp.sum(
        jnp.where(matches, jnp.arange(table_len, dtype=jnp.int32)[None, :], 0), axis=1
    )
    owners = jnp.repeat(entries // tail_pages, PAGE)
    tail_pos = jnp.repeat(entries % tail_pages, PAGE) * PAGE + jnp.tile(
        jnp.arange(PAGE, dtype=jnp.int32), slot_count
    )
    tail_mask = (owners[None, :] == jnp.arange(rows_req, dtype=jnp.int32)[:, None]) & (
        tail_pos[None, :] < tail_lengths[:, None]
    )
    tail_mask = tail_mask[:, None, None, None, :]
    pool_keys = tail_keys[0].reshape(pool_rows, KV, HD)
    pool_values = tail_values[0].reshape(pool_rows, KV, HD)
    tail_scores = jnp.einsum(
        "rskgd,pkd->rskgp", query_groups, pool_keys, preferred_element_type=jnp.float32
    )
    tail_scores = jnp.where(tail_mask, tail_scores, NEGATIVE)
    block_top = jnp.maximum(jnp.max(prompt_scores, axis=(4, 5)), jnp.max(tail_scores, axis=4))
    prompt_probs = jnp.where(prompt_mask, jnp.exp(prompt_scores - block_top[..., None, None]), 0.0)
    tail_probs = jnp.where(tail_mask, jnp.exp(tail_scores - block_top[..., None]), 0.0)
    block_total = jnp.sum(prompt_probs, axis=(4, 5)) + jnp.sum(tail_probs, axis=4)
    block_accum = jnp.einsum(
        "rskgcp,cpkd->rskgd",
        prompt_probs.astype(jnp.bfloat16),
        cache_values,
        preferred_element_type=jnp.float32,
    )
    block_accum = block_accum + jnp.einsum(
        "rskgp,pkd->rskgd",
        tail_probs.astype(jnp.bfloat16),
        pool_values,
        preferred_element_type=jnp.float32,
    )
    new_scores = jnp.einsum(
        "rskgd,rukd->rskgu", query_groups, keys_new, preferred_element_type=jnp.float32
    )
    causal = (jnp.arange(step_count)[:, None] >= jnp.arange(step_count)[None, :])[
        None, :, None, None, :
    ]
    new_scores = jnp.where(causal, new_scores, NEGATIVE)
    attn_rows_dev = w_out.shape[0]
    top_max = lax.pmax(block_top, "seq")
    rescale = jnp.exp(block_top - top_max)
    total_sum, accumulated = lax.psum(
        (block_total * rescale, block_accum * rescale[..., None]), "seq"
    )
    highest = jnp.maximum(top_max, jnp.max(new_scores, axis=4))
    carried = jnp.exp(top_max - highest)
    new_probs = jnp.where(causal, jnp.exp(new_scores - highest[..., None]), 0.0)
    denominator = total_sum * carried + jnp.sum(new_probs, axis=4)
    numerator = accumulated * carried[..., None] + jnp.einsum(
        "rskgu,rukd->rskgd", new_probs, values_new.astype(jnp.float32)
    )
    attention = (
        (numerator / denominator[..., None])
        .astype(jnp.bfloat16)
        .reshape(rows_req, step_count, H * HD)
    )
    attention_cols = lax.dynamic_slice_in_dim(
        attention, seq_index * attn_rows_dev, attn_rows_dev, 2
    ).reshape(tokens, attn_rows_dev)
    out_part = jnp.dot(attention_cols, out_full, preferred_element_type=jnp.float32)
    attn_out = lax.psum(out_part, "seq")
    residual = hidden.reshape(tokens, D) + normalize(attn_out) * post_attn_gain
    ffn_in = (normalize(residual) * ffn_gain).astype(jnp.bfloat16)
    gate_out = jnp.dot(ffn_in, gate_full, preferred_element_type=jnp.float32)
    up_out = jnp.dot(ffn_in, up_full, preferred_element_type=jnp.float32)
    activated = (jax.nn.gelu(gate_out, approximate=True) * up_out).astype(jnp.bfloat16)
    down_part = jnp.dot(activated, down_full, preferred_element_type=jnp.float32)
    down_out = lax.psum(down_part, "seq")
    layer_out = residual + normalize(down_out) * post_ffn_gain
    return layer_out.astype(jnp.bfloat16).reshape(rows_req, step_count, D)


def solution(mesh):
    return jax.shard_map(
        on_device,
        mesh=mesh,
        in_specs=(
            P("req", None, None),
            P(),
            P(),
            P(),
            P(),
            P(),
            P(),
            P("seq", "req"),
            P("seq", "req"),
            P("req", "seq"),
            P("req", "seq"),
            P("seq", "req"),
            P("req", "seq", None),
            P("req", "seq", None),
            P("req", "seq", None),
            P("req", "seq", None),
            P("req"),
            P("req"),
            P("req"),
            P("req", None),
        ),
        out_specs=P("req", None, None),
        check_vma=False,
    )
```

profile of v0, /device:TPU:2, one launch (start us, length us, event | category | flops | bytes accessed | tf_op | source)
XLA Modules:
  0.0 1219.5 jit_solution(10066826392859031519)
XLA Ops:
  6.5 1.1 convert_element_type.35
  7.8 0.7 copy-done.11
  8.6 15.6 %all_gather.15 = bf16[32,3072]{1,0:T(8,128)(2,1)S(1)} all-gather(bf16[32,384]{1,0:T(8,128)(2,1)S(1)} %copy-done.11), channel_id=1, replica_groups=mesh['seq'=64,'req'=8] {'req'}, dimensions={1}, use_global_device_ids=true | all-gather | bytes 221184 | tf_op jit(solution)/shard_map/all_gather | solution.py:54
  24.1 0.8 dynamic-slice
  25.0 0.2 fusion.68
  25.2 0.2 reshape.248
  25.5 1.4 copy.120
  27.0 0.6 copy-done.15
  27.8 13.0 %all_gather.16 = bf16[32,2048]{1,0:T(8,128)(2,1)S(1)} all-gather(bf16[32,256]{1,0:T(8,128)(2,1)S(1)} %copy-done.12), channel_id=1, replica_groups=mesh['seq'=64,'req'=8] {'req'}, dimensions={1}, use_global_device_ids=true | all-gather | bytes 147456 | tf_op jit(solution)/shard_map/all_gather | solution.py:55
  41.2 0.9 copy-done.4
  42.1 0.9 copy-done.5
  43.1 0.9 copy-done.6
  44.0 0.6 copy-done.20
  44.8 0.6 copy-done.19
  45.5 142.4 %all-reduce.5.cloned.1.call-done = f32[16,4,3072]{2,0,1:T(8,128)} async-done(((f32[16,4,3072]{2,0,1:T(8,128)}), f32[16,4,3072]{2,0,1:T(8,128)}) %all-reduce.5.cloned.1.call-update) | async-done | bytes 786448 | tf_op jit(solution)/shard_map/psum | solution.py:61
  187.8 1.1 slice_multiply_fusion
  189.4 0.4 reshape.249
  189.8 0.7 copy-done.16
  190.6 0.4 fusion.65
  191.1 0.3 fusion.66
  191.4 277.1 %pmax.7 = f32[16,4,2,4]{0,3,1,2:T(4,128)S(1)} all-reduce(f32[16,4,2,4]{0,3,1,2:T(4,128)S(1)} %max.16), channel_id=1, replica_groups=mesh['seq'=64,'req'=8] {'seq'}, use_global_device_ids=true, to_apply=%region_6.7 | all-reduce | flops 512 | bytes 4096 | tf_op jit(solution)/shard_map/pmax | solution.py:133
  468.6 0.3 fusion.13
  468.8 0.3 fusion.11
  469.1 1.0 fusion.64
  470.4 0.6 copy-done.17
  471.2 1.3 fusion.67
  472.8 0.3 fusion.30
  473.2 273.9 %psum.37 = f32[16,4,2,4]{0,3,1,2:T(4,128)S(1)} all-reduce(f32[16,4,2,4]{0,3,1,2:T(4,128)S(1)} %bitcast.93), channel_id=1, replica_groups=mesh['seq'=64,'req'=8] {'seq'}, use_global_device_ids=true, to_apply=%region_13.14 | all-reduce | flops 512 | bytes 4096 | tf_op jit(solution)/shard_map/psum | solution.py:135
  747.2 0.3 convolution_bitcast_fusion
  747.4 1.1 fusion.3
  749.0 0.4 fusion.31
  749.5 149.1 %all-reduce.7.cloned.1.call-done = f32[16,4,2,4,256]{4,0,3,1,2:T(8,128)} async-done(((f32[16,4,2,4,256]{4,0,3,1,2:T(8,128)}), f32[16,4,2,4,256]{4,0,3,1,2:T(8,128)}) %all-reduce.7.cloned.1.call-update) | async-done | bytes 524304 | tf_op jit(solution)/shard_map/psum | solution.py:135
  898.6 1.4 fusion.8
  900.4 1.0 fusion.69
  901.5 0.8 copy-done.7
  902.3 13.1 %all_gather.17 = bf16[2048,128]{1,0:T(8,128)(2,1)S(1)} all-gather(bf16[256,128]{1,0:T(8,128)(2,1)S(1)} %copy-done.7), channel_id=1, replica_groups=mesh['seq'=64,'req'=8] {'req'}, dimensions={0}, use_global_device_ids=true | all-gather | bytes 589824 | tf_op jit(solution)/shard_map/all_gather | solution.py:56
  915.4 0.8 copy-done.8
  916.2 13.2 %all_gather.18 = bf16[2048,128]{1,0:T(8,128)(2,1)S(1)} all-gather(bf16[256,128]{1,0:T(8,128)(2,1)S(1)} %copy-done.8), channel_id=1, replica_groups=mesh['seq'=64,'req'=8] {'req'}, dimensions={0}, use_global_device_ids=true | all-gather | bytes 589824 | tf_op jit(solution)/shard_map/all_gather | solution.py:57
  929.4 13.2 %all_gather.19 = bf16[128,2048]{1,0:T(8,128)(2,1)S(1)} all-gather(bf16[128,256]{1,0:T(8,128)(2,1)S(1)} %copy-done.9), channel_id=1, replica_groups=mesh['seq'=64,'req'=8] {'req'}, dimensions={1}, use_global_device_ids=true | all-gather | bytes 589824 | tf_op jit(solution)/shard_map/all_gather | solution.py:58
  942.6 111.9 %all-reduce.9.cloned.1.call-done = f32[64,2048]{1,0:T(8,128)} async-done(((f32[64,2048]{1,0:T(8,128)}), f32[64,2048]{1,0:T(8,128)}) %all-reduce.9.cloned.1.call-update) | async-done | bytes 524304 | tf_op jit(solution)/shard_map/psum | solution.py:154
  1054.6 1.2 multiply_reduce_fusion.2
  1055.9 0.3 multiply_reduce_fusion.1
  1056.1 0.4 copy-done.10
  1056.6 0.3 fusion.63
  1056.8 1.3 fusion.6
  1058.1 152.6 %all-reduce.11.cloned.1.call-done = f32[64,2048]{1,0:T(8,128)} async-done(((f32[64,2048]{1,0:T(8,128)}), f32[64,2048]{1,0:T(8,128)}) %all-reduce.11.cloned.1.call-update) | async-done | bytes 524304 | tf_op jit(solution)/shard_map/psum | solution.py:161
  1210.7 1.2 multiply_reduce_fusion
  1212.1 0.8 reshape.256
  (86 shorter events, 4.0 us)
Async XLA Ops:
  6.5 181.3 %all-reduce.5.cloned.1.call-start = ((), (), s32[]{:S(2)}) async-start(), calls=%async_computation | async-start | bytes 1572864 | tf_op jit(solution)/shard_map/psum | solution.py:61
  6.5 1.1 copy-start
  7.8 0.7 copy-start.11
  26.8 0.7 copy-start.15
  26.8 0.9 copy-start.18
  26.8 14.2 %copy-start.3 = (bf16[1,256,512]{2,1,0:T(8,128)(2,1)S(1)}, bf16[1,256,512]{2,1,0:T(8,128)(2,1)}, u32[]{:S(2)}) copy-start(bf16[1,256,512]{2,1,0:T(8,128)(2,1)} %param.34) | copy-start | bytes 786436
  26.9 0.9 copy-start.12
  26.9 871.7 %all-reduce.7.cloned.1.call-start = ((), (), s32[]{:S(2)}) async-start(), calls=%async_computation.1 | async-start | bytes 1048576 | tf_op jit(solution)/shard_map/psum | solution.py:135
  41.1 1.0 copy-start.4
  42.0 1.0 copy-start.5
  43.0 0.9 copy-start.6
  44.0 0.7 copy-start.20
  44.7 0.7 copy-start.19
  189.7 0.7 copy-start.16
  470.4 0.7 copy-start.17
  748.6 306.0 %all-reduce.9.cloned.1.call-start = ((), (), s32[]{:S(2)}) async-start(), calls=%async_computation.2 | async-start | bytes 1048576 | tf_op jit(solution)/shard_map/psum | solution.py:154
  901.4 0.8 copy-start.7
  901.4 309.3 %all-reduce.11.cloned.1.call-start = ((), (), s32[]{:S(2)}) async-start(), calls=%async_computation.3 | async-start | bytes 1048576 | tf_op jit(solution)/shard_map/psum | solution.py:161
  915.4 0.8 copy-start.8
  916.2 13.2 %copy-start.9 = (bf16[128,256]{1,0:T(8,128)(2,1)S(1)}, bf16[128,256]{1,0:T(8,128)(2,1)}, u32[]{:S(2)}) copy-start(bf16[128,256]{1,0:T(8,128)(2,1)} %param.31) | copy-start | bytes 196612
  929.4 126.4 %copy-start.13 = (f32[2048]{0:T(1024)S(1)}, f32[2048]{0:T(1024)}, u32[]{:S(2)}) copy-start(f32[2048]{0:T(1024)} %param.24) | copy-start | bytes 24580
  1054.6 1.3 copy-start.2
  1055.9 0.7 copy-start.10
  1058.1 153.8 %copy-start.14 = (f32[2048]{0:T(1024)S(1)}, f32[2048]{0:T(1024)}, u32[]{:S(2)}) copy-start(f32[2048]{0:T(1024)} %param.26) | copy-start | bytes 24580
  1210.7 1.3 copy-start.1
Sparse Core Ops, SparseCore 0:
  27.0 160.8 all-reduce.4
  748.7 149.8 all-reduce.6
  902.1 152.4 all-reduce.8
  1058.3 152.3 all-reduce.10
where the time goes:
time: 1220 us
  blocking collectives  619 us (51%)
  waiting for transfers between devices  556 us (46%)
  local copies, waits for them, and re-layouts  14.7 us (1%)
  between operations  13.5 us (1%)
    pmax x1, blocking collectives, on_device(): top_max = lax.pmax(block_top, 'seq')  277 us
    psum x1, blocking collectives, on_device(): lax.psum((block_total * rescale, block_accum * rescale[..., None]), 'seq')  274 us
    psum x1, waiting for transfers between devices, on_device(): down_out = lax.psum(down_part, 'seq')  153 us
    psum x1, waiting for transfers between devices, on_device(): lax.psum((block_total * rescale, block_accum * rescale[..., None]), 'seq')  149 us
    psum x1, waiting for transfers between devices, on_device(): projected = lax.psum(qkv_part, 'seq').reshape(rows_req, step_count, QKV)  142 us
    psum x1, waiting for transfers between devices, on_device(): attn_out = lax.psum(out_part, 'seq')  112 us
  transfers between devices with their start and end apart: 4, of which 4 were waited for; matrix products, arithmetic and copies ran while one was open for 0% of the time, Pallas kernels for 0%

commit v1 on v0

--- a/solution.py
+++ b/solution.py
@@ -58,7 +58,7 @@
         lax.all_gather(w_down, "req", axis=1, tiled=True),
     )
     qkv_part = jnp.dot(normed_cols, qkv_full, preferred_element_type=jnp.float32)
-    projected = lax.psum(qkv_part, "seq").reshape(rows_req, step_count, QKV)
+    projected = jnp.sum(lax.all_gather(qkv_part, "seq"), axis=0).reshape(rows_req, step_count, QKV)
     queries = (
         normalize(projected[..., : H * HD].reshape(rows_req, step_count, H, HD)) * q_gain
     ).astype(jnp.bfloat16)

time: 1220 us -> 1390 us (1.14)
  waiting for transfers between devices: 556 us -> 698 us
  other arithmetic: 9.17 us -> 36.4 us
    all_gather x0 -> x1, waiting for transfers between devices: none -> 283 us  [on_device(): lax.all_gather(qkv_part, 'seq')]
    psum x1 -> x0, waiting for transfers between devices: 142 us -> none  [on_device(): projected = lax.psum(qkv_part, 'seq').reshape(rows_req, step_count, QKV)]
    reduce_sum x0 -> x1, other arithmetic: none -> 17.2 us  [on_device(): jnp.sum(lax.all_gather(qkv_part, 'seq'), axis=0)]
  transfers between devices with their start and end apart: 4 -> 4, of which waited for: 4 -> 4; matrix products, arithmetic and copies ran while one was open for 0% -> 1% of each run, Pallas kernels for 0% -> 0%
where the time goes in v1:
time: 1390 us
  waiting for transfers between devices  698 us (50%)
  blocking collectives  621 us (45%)
  other arithmetic  36.4 us (3%)
    all_gather x1, waiting for transfers between devices, on_device(): lax.all_gather(qkv_part, 'seq')  283 us
    pmax x1, blocking collectives, on_device(): top_max = lax.pmax(block_top, 'seq')  278 us
    psum x1, blocking collectives, on_device(): lax.psum((block_total * rescale, block_accum * rescale[..., None]), 'seq')  274 us
    psum x1, waiting for transfers between devices, on_device(): down_out = lax.psum(down_part, 'seq')  153 us
    psum x1, waiting for transfers between devices, on_device(): lax.psum((block_total * rescale, block_accum * rescale[..., None]), 'seq')  149 us
    psum x1, waiting for transfers between devices, on_device(): attn_out = lax.psum(out_part, 'seq')  113 us
  transfers between devices with their start and end apart: 4, of which 4 were waited for; matrix products, arithmetic and copies ran while one was open for 1% of the time, Pallas kernels for 0%

profile of v1, /device:TPU:2, one launch (start us, length us, event | category | flops | bytes accessed | tf_op | source)
XLA Modules:
  0.0 1389.7 jit_solution(4517494410401130023)
XLA Ops:
  6.5 1.1 convert_element_type.35
  7.6 1.2 multiply_reduce_fusion.3
  8.8 15.8 %all_gather.21 = bf16[32,3072]{1,0:T(8,128)(2,1)S(1)} all-gather(bf16[32,384]{1,0:T(8,128)(2,1)} %param.27), channel_id=1, replica_groups=mesh['seq'=64,'req'=8] {'req'}, dimensions={1}, use_global_device_ids=true | all-gather | bytes 221184 | tf_op jit(solution)/shard_map/all_gather | solution.py:54
  24.6 0.8 dynamic-slice
  25.4 1.1 fusion.68
  26.7 0.9 select_reduce_fusion
  27.5 0.7 and_select_fusion.1
  28.5 1.0 reshape_squeeze.6
  29.5 1.0 reshape.250
  30.6 1.0 reshape.251
  31.6 1.0 reshape_squeeze.7
  32.6 13.2 all_gather.24
  45.8 0.6 iota_compare_fusion.1
  46.4 0.7 broadcast_compare_fusion
  47.2 0.7 broadcast_and_fusion
  47.8 1.3 fusion.53
  49.1 283.3 %all-gather.3.cloned.1.call-done = f32[4096,3072]{1,0:T(8,128)} async-done(((f32[64,3072]{1,0:T(8,128)}), f32[4096,3072]{1,0:T(8,128)}) %all-gather.3.cloned.1.call-update) | async-done | bytes 50331664 | tf_op jit(solution)/shard_map/all_gather | solution.py:61
  332.4 17.2 %reduce_sum.109 = f32[64,3072]{1,0:T(8,128)S(1)} reduce(f32[64,64,3072]{2,1,0:T(8,128)} %bitcast.61, f32[]{:T(128)} %constant.69.clone.1), dimensions={0}, to_apply=%region_1.0 | reduce | flops 12386304 | bytes 51118084 | tf_op jit(solution)/shard_map/reduce_sum | solution.py:61
  350.2 0.3 mul.206
  350.7 0.4 reshape.266
  351.2 1.0 fusion.10
  352.2 1.2 fusion.65
  353.4 1.0 fusion.66
  354.4 277.7 %pmax.7 = f32[16,4,2,4]{0,3,1,2:T(4,128)S(1)} all-reduce(f32[16,4,2,4]{0,3,1,2:T(4,128)S(1)} %max.16), channel_id=1, replica_groups=mesh['seq'=64,'req'=8] {'seq'}, use_global_device_ids=true, to_apply=%region_6.7 | all-reduce | flops 512 | bytes 4096 | tf_op jit(solution)/shard_map/pmax | solution.py:133
  632.1 0.9 fusion.13
  633.1 1.0 fusion.11
  634.6 0.8 fusion.35
  635.4 2.0 fusion.67
  637.6 0.9 fusion.30
  638.7 273.9 %psum.29 = f32[16,4,2,4]{0,3,1,2:T(4,128)S(1)} all-reduce(f32[16,4,2,4]{0,3,1,2:T(4,128)S(1)} %bitcast.81), channel_id=1, replica_groups=mesh['seq'=64,'req'=8] {'seq'}, use_global_device_ids=true, to_apply=%region_13.14 | all-reduce | flops 512 | bytes 4096 | tf_op jit(solution)/shard_map/psum | solution.py:135
  912.7 1.0 convolution_bitcast_fusion
  913.6 1.8 fusion.3
  916.1 1.1 fusion.31
  917.2 148.7 %all-reduce.4.cloned.1.call-done = f32[16,4,2,4,256]{4,0,3,1,2:T(8,128)} async-done(((f32[16,4,2,4,256]{4,0,3,1,2:T(8,128)}), f32[16,4,2,4,256]{4,0,3,1,2:T(8,128)}) %all-reduce.4.cloned.1.call-update) | async-done | bytes 524304 | tf_op jit(solution)/shard_map/psum | solution.py:135
  1065.9 1.4 fusion.8
  1067.7 1.0 fusion.69
  1068.8 13.3 all_gather.25
  1082.2 13.3 all_gather.26
  1095.5 13.3 all_gather.27
  1108.8 113.1 %all-reduce.6.cloned.1.call-done = f32[64,2048]{1,0:T(8,128)} async-done(((f32[64,2048]{1,0:T(8,128)}), f32[64,2048]{1,0:T(8,128)}) %all-reduce.6.cloned.1.call-update) | async-done | bytes 524304 | tf_op jit(solution)/shard_map/psum | solution.py:154
  1221.9 1.2 multiply_reduce_fusion.2
  1223.1 1.3 multiply_reduce_fusion.1
  1224.5 1.0 fusion.63
  1225.4 2.0 fusion.6
  1227.4 152.6 %all-reduce.8.cloned.1.call-done = f32[64,2048]{1,0:T(8,128)} async-done(((f32[64,2048]{1,0:T(8,128)}), f32[64,2048]{1,0:T(8,128)}) %all-reduce.8.cloned.1.call-update) | async-done | bytes 524304 | tf_op jit(solution)/shard_map/psum | solution.py:161
  1380.0 1.2 multiply_reduce_fusion
  1381.2 1.2 add_convert_fusion
  1382.4 0.8 reshape.256
  (50 shorter events, 3.4 us)
Async XLA Ops:
  6.5 1075.6 %copy-start = (bf16[16,4,2048]{2,1,0:T(4,128)(2,1)S(1)}, bf16[16,4,2048]{2,1,0:T(4,128)(2,1)}, u32[]{:S(2)}) copy-start(bf16[16,4,2048]{2,1,0:T(4,128)(2,1)} %param.20) | copy-start | bytes 786436
  6.5 325.9 %all-gather.3.cloned.1.call-start = ((), (), s32[]{:S(2)}) async-start(), calls=%async_computation.3 | async-start | bytes 51118080 | tf_op jit(solution)/shard_map/all_gather | solution.py:61
  26.6 1039.3 %all-reduce.4.cloned.1.call-start = ((), (), s32[]{:S(2)}) async-start(), calls=%async_computation | async-start | bytes 1048576 | tf_op jit(solution)/shard_map/psum | solution.py:135
  915.4 306.5 %all-reduce.6.cloned.1.call-start = ((), (), s32[]{:S(2)}) async-start(), calls=%async_computation.1 | async-start | bytes 1048576 | tf_op jit(solution)/shard_map/psum | solution.py:154
  1068.8 311.2 %all-reduce.8.cloned.1.call-start = ((), (), s32[]{:S(2)}) async-start(), calls=%async_computation.2 | async-start | bytes 1048576 | tf_op jit(solution)/shard_map/psum | solution.py:161
Sparse Core Ops, SparseCore 0:
  26.7 305.6 all-gather.2
  915.5 150.3 all-reduce.3
  1069.5 152.4 all-reduce.5
  1227.6 152.3 all-reduce.7
